TPU v7x, 32 devices: a whole 2x2x4 slice. The times are simulated.
32 devices in a mesh: row: 4 (over x, core), col: 8 (over z, y).
Axes of the slice: x: 2, y: 2, z: 4, core: 2. Of those that a mesh axis runs over, the one named last changes fastest.
Arguments:
- p_valence: bfloat16 [4096, 4096], P('row', 'col'), as said below
- p_conduction: bfloat16 [4096, 4096], P('row', 'col'), as said below
- trial_vectors: bfloat16 [2, 4096, 4096], P(None, 'row', 'col'), may hold values from -6 to 6
- mask_valence: int32 [32, 32], replicated, may hold values from 0 to 1, as said below
- mask_conduction: int32 [32, 32], replicated, may hold values from 0 to 1, as said below
- mask_trial: int32 [32, 32], replicated, may hold values 0 or 1
- orbitals: bfloat16 [32, 128, 8192], P('row'), may hold values from -0.29882812 to 0.29882812
- sphere_starts: int32 [32], replicated, may hold values from 0 to 16, as said below
Outputs:
- kernel: bfloat16 [2, 4096, 4096], P(None, 'row', 'col')
- density: float32 [2, 16384], P(None, ('row', 'col'))
Inputs may be any that keep to these rules, and one draw needn't show every extreme that they name: `mask_valence`: symmetric, ones on the block diagonal and next to it. `mask_conduction`: symmetric, ones on the block diagonal and next to it. `p_valence`: symmetric. `p_conduction`: symmetric. `sphere_starts`: the first block's start is 0 and the last block's 32 - 16.
All inputs are finite; a program needn't handle non-finite values.
Results may differ from a plain program's by a relative error of at most 0.0049.
Values may be sent and summed in bfloat16 or wider, within the bound.
A program may use at most 320 MiB of HBM per device.

v0:
```python
import jax
import jax.numpy as jnp
from jax import lax
from jax.sharding import PartitionSpec as P

BS = 128
SPAN = 16
SP = 512


def broadcast(x, axis, root):
    mine = lax.axis_index(axis) == root
    return lax.psum(jnp.where(mine, x, jnp.zeros_like(x)), axis)


def masked(values, block_mask, row_index, col_index):
    leading_dims = values.shape[:-2]
    row_blocks = values.shape[-2] // BS
    col_blocks = values.shape[-1] // BS
    tile_mask = lax.dynamic_slice(
        block_mask, (row_index * row_blocks, col_index * col_blocks), (row_blocks, col_blocks)
    ).astype(values.dtype)
    shaped = values.reshape(leading_dims + (row_blocks, BS, col_blocks, BS))
    return (shaped * tile_mask[:, None, :, None]).reshape(values.shape)


def local(
    p_valence,
    p_conduction,
    trial_vectors,
    mask_valence,
    mask_conduction,
    mask_trial,
    orbitals,
    sphere_starts,
):
    row_index = lax.axis_index("row")
    col_index = lax.axis_index("col")
    valence = masked(p_valence, mask_valence, row_index, col_index)
    conduction = masked(p_conduction, mask_conduction, row_index, col_index)
    trials = masked(trial_vectors, mask_trial, row_index, col_index)
    vector_count = trials.shape[0]
    local_rows = trials.shape[1]
    local_cols = trials.shape[2]
    panels = lax.all_gather(trials, "col", axis=2, tiled=True)
    response = jnp.einsum(
        "vik,kj->vij",
        panels,
        lax.all_gather(conduction, "row", axis=0, tiled=True),
        preferred_element_type=jnp.float32,
    )
    response_half = response.astype(jnp.bfloat16)
    gathered = lax.all_gather(response_half, "row", axis=1, tiled=True)
    kernel_sum = jnp.einsum(
        "ik,vkj->vij",
        lax.all_gather(valence, "col", axis=1, tiled=True),
        gathered,
        preferred_element_type=jnp.float32,
    )
    kernel = masked(kernel_sum, mask_trial, row_index, col_index).astype(jnp.bfloat16)
    row_blocks = local_rows // BS
    col_blocks = local_cols // BS
    ratio = lax.axis_size("col") // lax.axis_size("row")
    own_part = lax.dynamic_slice_in_dim(orbitals, col_index % ratio * col_blocks, col_blocks, 0)
    partner = broadcast(own_part, "row", col_index // ratio)
    partner_padded = jnp.pad(
        partner.reshape(col_blocks, BS, SPAN, SP), ((0, 0), (0, 0), (SPAN, SPAN), (0, 0))
    )
    starts_rows = lax.dynamic_slice_in_dim(sphere_starts, row_index * row_blocks, row_blocks, 0)
    starts_cols = lax.dynamic_slice_in_dim(sphere_starts, col_index * col_blocks, col_blocks, 0)
    offsets = jnp.clip(starts_rows[:, None] - starts_cols[None, :] + SPAN, 0, 2 * SPAN)

    def take_frame(orbital_block, offset):
        return lax.dynamic_slice_in_dim(orbital_block, offset, SPAN, 1)

    def frames_for_row(offset_row):
        return jax.vmap(take_frame)(partner_padded, offset_row)

    frames = jax.vmap(frames_for_row)(offsets).reshape(row_blocks, col_blocks, BS, SPAN * SP)
    kernel_blocks = kernel.reshape(vector_count, row_blocks, BS, col_blocks, BS).transpose(
        0, 1, 3, 2, 4
    )
    applied = jnp.einsum(
        "vabmn,abnp->vamp", kernel_blocks, frames, preferred_element_type=jnp.float32
    )
    contrib = jnp.sum(orbitals[None] * applied, axis=2)
    slab_count = lax.axis_size("row") * lax.axis_size("col")
    density_grid = jnp.zeros((vector_count, slab_count, SP), jnp.float32)
    zero_index = jnp.zeros((), jnp.int32)
    for local_block in range(row_blocks):
        begin_slab = starts_rows[local_block]
        current = lax.dynamic_slice(
            density_grid, (zero_index, begin_slab, zero_index), (vector_count, SPAN, SP)
        )
        update = current + contrib[:, local_block].reshape(vector_count, SPAN, SP)
        density_grid = lax.dynamic_update_slice(
            density_grid, update, (zero_index, begin_slab, zero_index)
        )
    own_slab = lax.psum_scatter(density_grid, ("row", "col"), scatter_dimension=1, tiled=True)
    density = own_slab.reshape(vector_count, SP)
    return (kernel, density)


def solution(mesh):
    placed = (
        P("row", "col"),
        P("row", "col"),
        P(None, "row", "col"),
        P(),
        P(),
        P(),
        P("row", None, None),
        P(),
    )
    return jax.shard_map(
        local,
        mesh=mesh,
        in_specs=placed,
        out_specs=(P(None, "row", "col"), P(None, ("row", "col"))),
        check_vma=False,
    )
```

profile of v0, /device:TPU:0, one launch (start us, length us, event | category | flops | bytes accessed | tf_op | source)
XLA Modules:
  0.0 935.6 jit_solution(7683359424325019603)
XLA Ops:
  13.9 7.4 dynamic-slice_select_fusion
  21.2 11.8 %copy.28 = bf16[64,8,16,512]{3,2,1,0:T(8,128)(2,1)} copy(bf16[64,8,16,512]{3,1,2,0:T(8,128)(2,1)} %bitcast.123) | data formatting | bytes 16777216
  35.6 18.6 %convert_element_type.30 = f32[8,128,8192]{2,1,0:T(8,128)} convert(bf16[8,128,8192]{2,1,0:T(8,128)(2,1)} %param.14) | non-fusion elementwise | flops 8388608 | bytes 50331648 | tf_op jit(solution)/shard_map/convert_element_type | solution.py:86
  65.0 213.2 %all-gather.5.cloned.1.call-done = bf16[2,1024,4096]{2,1,0:T(8,128)(2,1)} async-done(((bf16[2,1024,512]{2,1,0:T(8,128)(2,1)}), bf16[2,1024,4096]{2,1,0:T(8,128)(2,1)}) %all-gather.5.cloned.1.call-update) | async-done | bytes 16777232 | tf_op jit(solution)/shard_map/all_gather | solution.py:45
  278.2 14.5 %fusion.13 = bf16[2,1024,512]{2,1,0:T(8,128)(2,1)} fusion(bf16[2,1024,4096]{2,1,0:T(8,128)(2,1)} %all-gather.5.cloned.1.call-done, bf16[4096,512]{1,0:T(8,128)(2,1)} %all-gather.7.cloned.1.call-done), kind=kOutput, calls=%fused_computation.15 | convolution fusion | flops 8590983168 | bytes 23068672 | tf_op jit(solution)/shard_map/vik,kj->vij/dot_general | solution.py:46
  298.9 132.9 %all-reduce.5.cloned.1.call-done = bf16[4,128,16,512]{3,2,1,0:T(8,128)(2,1)} async-done(((bf16[4,128,16,512]{3,2,1,0:T(8,128)(2,1)}), bf16[4,128,16,512]{3,2,1,0:T(8,128)(2,1)}) %all-reduce.5.cloned.1.call-update) | async-done | bytes 8388624 | tf_op jit(solution)/shard_map/psum | solution.py:13
  431.8 12.1 %pad.4 = bf16[4,128,48,512]{3,2,1,0:T(8,128)(2,1)} pad(bf16[4,128,16,512]{3,2,1,0:T(8,128)(2,1)} %all-reduce.5.cloned.1.call-done, bf16[]{:T(256)} %constant.48.clone.1), padding=0_0x0_0x16_16x0_0 | pad | bytes 33554432 | tf_op jit(solution)/shard_map/jit(_pad)/pad | solution.py:66
  443.9 204.5 %while.1 = (s32[]{:T(128)}, bf16[4,128,48,512]{3,2,1,0:T(8,128)(2,1)}, s32[32,4]{0,1:T(4,128)S(1)}, bf16[32,128,16,512]{3,2,1,0:T(8,128)(2,1)}, s32[]{:T(128)}) while((s32[]{:T(128)}, bf16[4,128,48,512]{3,2,1,0:T(8,128)(2,1)}, s32[32,4]{0,1:T(4,128)S(1)}, bf16[32,128,16,512]{3,2,1,0:T(8,128)(2,1)}, s32[]{:T(128)}) %tuple.42), condition=%wide.while_cond, body=%wide.while_body.sunk | while | flops 2 | bytes 4195953 | solution.py:74
  457.3 5.8 dynamic-slice_dynamic-update-slice_fusion.2
  463.7 5.7 dynamic-slice_dynamic-update-slice_fusion.2
  470.1 5.7 dynamic-slice_dynamic-update-slice_fusion.2
  482.9 5.7 dynamic-slice_dynamic-update-slice_fusion.2
  514.8 5.7 dynamic-slice_dynamic-update-slice_fusion.2
  521.2 5.7 dynamic-slice_dynamic-update-slice_fusion.2
  534.0 5.8 dynamic-slice_dynamic-update-slice_fusion.2
  553.1 5.7 dynamic-slice_dynamic-update-slice_fusion.2
  565.8 6.2 dynamic-slice_dynamic-update-slice_fusion.2
  572.7 5.7 dynamic-slice_dynamic-update-slice_fusion.2
  591.7 5.8 dynamic-slice_dynamic-update-slice_fusion.2
  604.6 5.7 dynamic-slice_dynamic-update-slice_fusion.2
  648.4 98.3 %reshape.126 = bf16[8,4,128,8192,1]{3,2,1,0,4:T(8,128)(2,1)} reshape(bf16[32,128,16,512]{3,2,1,0:T(8,128)(2,1)} %get-tuple-element.9) | data formatting | bytes 134217728 | tf_op jit(solution)/shard_map/reshape | solution.py:79
  746.8 13.8 %fusion.7 = bf16[2,1024,512]{1,2,0:T(8,128)(2,1)S(1)} fusion(bf16[2,4096,512]{2,1,0:T(8,128)(2,1)} %all-gather.9.cloned.1.call-done, bf16[1024,4096]{1,0:T(8,128)(2,1)} %all-gather.11.cloned.1.call-done, f32[1024,512]{0,1:T(8,128)S(1)} %bitcast.131), kind=kOutput, calls=%fused_computation.10 | convolution fusion | flops 8592031744 | bytes 20971520 | tf_op jit(solution)/shard_map/ik,vkj->vij/dot_general | solution.py:54
  765.7 33.2 %fusion = f32[2,8,8192]{2,0,1:T(2,128)S(1)} fusion(f32[8,128,8192]{2,1,0:T(8,128)} %convert_element_type.30, bf16[8,4,128,8192,1]{3,2,1,0,4:T(8,128)(2,1)} %reshape.126, bf16[2,8,128,4,128]{4,2,3,0,1:T(8,128)(2,1)S(1)} %copy.18), kind=kOutput, calls=%fused_computation.3 | convolution fusion | flops 17213292544 | bytes 103284736 | tf_op jit(solution)/shard_map/vabmn,abnp->vamp/dot_general | solution.py:83
  806.6 120.9 %all-reduce.7.cloned.1.call-done = f32[2,32,512]{2,0,1:T(2,128)} async-done(((f32[2,32,512]{2,0,1:T(2,128)}), f32[2,32,512]{2,0,1:T(2,128)}) %all-reduce.7.cloned.1.call-update) | async-done | bytes 131088
  (151 shorter events, 160.0 us)
Async XLA Ops:
  7.2 5.1 copy-start.1
  7.2 57.8 %all-gather.7.cloned.1.call-start = ((), (), s32[]{:S(2)}) async-start(), calls=%async_computation.1 | async-start | bytes 5242880 | tf_op jit(solution)/shard_map/all_gather | solution.py:49
  10.9 267.3 %all-gather.5.cloned.1.call-start = ((), (), s32[]{:S(2)}) async-start(), calls=%async_computation | async-start | bytes 18874368 | tf_op jit(solution)/shard_map/all_gather | solution.py:45
  13.8 418.0 %all-reduce.5.cloned.1.call-start = ((), (), s32[]{:S(2)}) async-start(), calls=%async_computation.4 | async-start | bytes 16777216 | tf_op jit(solution)/shard_map/psum | solution.py:13
  33.0 1.2 copy-start.2
  33.0 2.5 copy-start.3
  33.0 713.7 %all-gather.11.cloned.1.call-start = ((), (), s32[]{:S(2)}) async-start(), calls=%async_computation.3 | async-start | bytes 9437184 | tf_op jit(solution)/shard_map/all_gather | solution.py:56
  35.4 711.3 %all-gather.9.cloned.1.call-start = ((), (), s32[]{:S(2)}) async-start(), calls=%async_computation.2 | async-start | bytes 10485760 | tf_op jit(solution)/shard_map/all_gather | solution.py:53
  292.8 634.7 %all-reduce.7.cloned.1.call-start = ((), (), s32[]{:S(2)}) async-start(), calls=%async_computation.5 | async-start | bytes 262144
  760.5 2.0 copy-start
Sparse Core Ops, SparseCore 0:
  11.0 37.2 all-gather.6
  50.9 227.2 all-gather.4
  280.7 151.0 all-reduce.4
  433.7 125.0 all-gather.10
  560.8 56.4 all-gather.8
  802.8 124.6 all-reduce.6
where the time goes:
time: 941 us; the launch traced here: 936 us
  waiting for transfers between devices  467 us (50%)
  local copies, waits for them, and re-layouts  344 us (37%)
  matrix products  61.5 us (7%)
  other arithmetic  32.9 us (3%)
  between operations  29.5 us (3%)
    all_gather x1, waiting for transfers between devices, local(): panels = lax.all_gather(trials, 'col', axis=2, tiled=True)  213 us
    gather x96, local copies, waits for them, and re-layouts  204 us
    psum x1, waiting for transfers between devices, broadcast(): return lax.psum(jnp.where(mine, x, jnp.zeros_like(x)), axis)  133 us
    unnamed x7, waiting for transfers between devices  121 us
    reshape x1, local copies, waits for them, and re-layouts, local(): jax.vmap(frames_for_row)(offsets)  98.3 us
    dot_general x1, matrix products, local(): jnp.einsum('vabmn,abnp->vamp', kernel_blocks, frames, preferred_element_t...  33.2 us
    unnamed x15, local copies, waits for them, and re-layouts  19.2 us
  transfers between devices with their start and end apart: 6, of which 3 were waited for; matrix products, arithmetic and copies ran while one was open for 40% of the time, Pallas kernels for 0%

commit v1 on v0

--- a/solution.py
+++ b/solution.py
@@ -10,7 +10,7 @@
 
 def broadcast(x, axis, root):
     mine = lax.axis_index(axis) == root
-    return lax.psum(jnp.where(mine, x, jnp.zeros_like(x)), axis)
+    return jnp.sum(lax.all_gather(jnp.where(mine, x, jnp.zeros_like(x)), axis), axis=0)
 
 
 def masked(values, block_mask, row_index, col_index):

time: 941 us -> 1180 us (1.25)
  waiting for transfers between devices: 467 us -> 693 us
  other arithmetic: 32.9 us -> 49.4 us
    all_gather x0 -> x1, waiting for transfers between devices: none -> 183 us  [broadcast(): lax.all_gather(jnp.where(mine, x, jnp.zeros_like(x)), axis)]
    psum x1 -> x0, waiting for transfers between devices: 133 us -> none  [broadcast(): return lax.psum(jnp.where(mine, x, jnp.zeros_like(x)), axis)]
    all_gather x1, waiting for transfers between devices: 0.01 us -> 67.5 us  [local(): lax.all_gather(valence, 'col', axis=1, tiled=True)]
    all_gather x1, waiting for transfers between devices: 0.01 us -> 58.5 us  [local(): gathered = lax.all_gather(response_half, 'row', axis=1, tiled=True)]
    all_gather x1, waiting for transfers between devices: 0.01 us -> 32.8 us  [local(): lax.all_gather(conduction, 'row', axis=0, tiled=True)]
    all_gather x1, waiting for transfers between devices: 213 us -> 230 us  [local(): panels = lax.all_gather(trials, 'col', axis=2, tiled=True)]
    reduce_sum x0 -> x1, other arithmetic: none -> 16.6 us  [broadcast(): jnp.sum(lax.all_gather(jnp.where(mine, x, jnp.zeros_like(x)), axis), axis=0)]
  transfers between devices with their start and end apart: 6 -> 6, of which waited for: 3 -> 6; matrix products, arithmetic and copies ran while one was open for 40% -> 6% of each run, Pallas kernels for 0% -> 0%
where the time goes in v1:
time: 1180 us; the launch traced here: 1170 us
  waiting for transfers between devices  693 us (59%)
  local copies, waits for them, and re-layouts  340 us (29%)
  matrix products  61.5 us (5%)
  other arithmetic  49.4 us (4%)
  between operations  29.3 us (2%)
    all_gather x1, waiting for transfers between devices, local(): panels = lax.all_gather(trials, 'col', axis=2, tiled=True)  230 us
    gather x96, local copies, waits for them, and re-layouts  201 us
    all_gather x1, waiting for transfers between devices, broadcast(): lax.all_gather(jnp.where(mine, x, jnp.zeros_like(x)), axis)  183 us
    unnamed x7, waiting for transfers between devices  121 us
    reshape x1, local copies, waits for them, and re-layouts, local(): jax.vmap(frames_for_row)(offsets)  98.3 us
    all_gather x1, waiting for transfers between devices, local(): lax.all_gather(valence, 'col', axis=1, tiled=True)  67.5 us
    all_gather x1, waiting for transfers between devices, local(): gathered = lax.all_gather(response_half, 'row', axis=1, tiled=True)  58.5 us
    dot_general x1, matrix products, local(): jnp.einsum('vabmn,abnp->vamp', kernel_blocks, frames, preferred_element_t...  33.2 us
  transfers between devices with their start and end apart: 6, of which 6 were waited for; matrix products, arithmetic and copies ran while one was open for 6% of the time, Pallas kernels for 0%

profile of v1, /device:TPU:0, one launch (start us, length us, event | category | flops | bytes accessed | tf_op | source)
XLA Modules:
  0.0 1173.4 jit_solution(2301497623006115511)
XLA Ops:
  15.4 32.8 %all-gather.9.cloned.1.call-done = bf16[4096,512]{1,0:T(8,128)(2,1)} async-done(((bf16[1024,512]{1,0:T(8,128)(2,1)}), bf16[4096,512]{1,0:T(8,128)(2,1)}) %all-gather.9.cloned.1.call-update) | async-done | bytes 4194320 | tf_op jit(solution)/shard_map/all_gather | solution.py:49
  48.3 230.0 %all-gather.7.cloned.1.call-done = bf16[2,1024,4096]{2,1,0:T(8,128)(2,1)} async-done(((bf16[2,1024,512]{2,1,0:T(8,128)(2,1)}), bf16[2,1024,4096]{2,1,0:T(8,128)(2,1)}) %all-gather.7.cloned.1.call-update) | async-done | bytes 16777232 | tf_op jit(solution)/shard_map/all_gather | solution.py:45
  278.2 14.5 %fusion.13 = bf16[2,1024,512]{2,1,0:T(8,128)(2,1)} fusion(bf16[2,1024,4096]{2,1,0:T(8,128)(2,1)} %all-gather.7.cloned.1.call-done, bf16[4096,512]{1,0:T(8,128)(2,1)} %all-gather.9.cloned.1.call-done), kind=kOutput, calls=%fused_computation.15 | convolution fusion | flops 8590983168 | bytes 23068672 | tf_op jit(solution)/shard_map/vik,kj->vij/dot_general | solution.py:46
  292.9 7.1 dynamic-slice_select_fusion
  300.8 18.6 %convert_element_type.32 = f32[8,128,8192]{2,1,0:T(8,128)} convert(bf16[8,128,8192]{2,1,0:T(8,128)(2,1)} %param.14) | non-fusion elementwise | flops 8388608 | bytes 50331648 | tf_op jit(solution)/shard_map/convert_element_type | solution.py:86
  335.9 67.5 %all-gather.13.cloned.1.call-done = bf16[1024,4096]{1,0:T(8,128)(2,1)} async-done(((bf16[1024,512]{1,0:T(8,128)(2,1)}), bf16[1024,4096]{1,0:T(8,128)(2,1)}) %all-gather.13.cloned.1.call-update) | async-done | bytes 8388624 | tf_op jit(solution)/shard_map/all_gather | solution.py:56
  403.4 58.5 %all-gather.11.cloned.1.call-done = bf16[2,4096,512]{2,1,0:T(8,128)(2,1)} async-done(((bf16[2,1024,512]{2,1,0:T(8,128)(2,1)}), bf16[2,4096,512]{2,1,0:T(8,128)(2,1)}) %all-gather.11.cloned.1.call-update) | async-done | bytes 8388624 | tf_op jit(solution)/shard_map/all_gather | solution.py:53
  461.9 13.8 %fusion.7 = bf16[2,1024,512]{1,2,0:T(8,128)(2,1)S(1)} fusion(bf16[2,4096,512]{2,1,0:T(8,128)(2,1)} %all-gather.11.cloned.1.call-done, bf16[1024,4096]{1,0:T(8,128)(2,1)} %all-gather.13.cloned.1.call-done, f32[1024,512]{0,1:T(8,128)S(1)} %bitcast.133), kind=kOutput, calls=%fused_computation.10 | convolution fusion | flops 8592031744 | bytes 20971520 | tf_op jit(solution)/shard_map/ik,vkj->vij/dot_general | solution.py:54
  481.4 183.4 %all-gather.15.cloned.1.call-done = bf16[16,128,8192]{2,1,0:T(8,128)(2,1)} async-done(((bf16[4,128,8192]{2,1,0:T(8,128)(2,1)}), bf16[16,128,8192]{2,1,0:T(8,128)(2,1)}) %all-gather.15.cloned.1.call-update) | async-done | bytes 33554448 | tf_op jit(solution)/shard_map/all_gather | solution.py:13
  664.8 16.6 %reduce_sum.21 = bf16[4,128,8192]{2,1,0:T(8,128)(2,1)} reduce(bf16[4,4,128,8192]{3,2,1,0:T(8,128)(2,1)} %bitcast.124, bf16[]{:T(256)} %constant.49.clone.1), dimensions={0}, to_apply=%region_0.1 | reduce | flops 12582912 | bytes 41943040 | tf_op jit(solution)/shard_map/reduce_sum | solution.py:13
  681.5 11.1 copy.28
  692.6 11.4 pad.4
  704.0 201.4 %while.1 = (s32[]{:T(128)}, bf16[4,128,48,512]{3,2,1,0:T(8,128)(2,1)}, s32[32,4]{0,1:T(4,128)S(1)}, bf16[32,128,16,512]{3,2,1,0:T(8,128)(2,1)}, s32[]{:T(128)}) while((s32[]{:T(128)}, bf16[4,128,48,512]{3,2,1,0:T(8,128)(2,1)}, s32[32,4]{0,1:T(4,128)S(1)}, bf16[32,128,16,512]{3,2,1,0:T(8,128)(2,1)}, s32[]{:T(128)}) %tuple.42), condition=%wide.while_cond, body=%wide.while_body.sunk | while | flops 2 | bytes 4195953 | solution.py:74
  717.2 5.7 dynamic-slice_dynamic-update-slice_fusion.2
  729.8 5.7 dynamic-slice_dynamic-update-slice_fusion.2
  780.2 5.7 dynamic-slice_dynamic-update-slice_fusion.2
  792.8 5.7 dynamic-slice_dynamic-update-slice_fusion.2
  811.6 5.7 dynamic-slice_dynamic-update-slice_fusion.2
  830.5 5.7 dynamic-slice_dynamic-update-slice_fusion.2
  862.0 5.7 dynamic-slice_dynamic-update-slice_fusion.2
  880.9 5.7 dynamic-slice_dynamic-update-slice_fusion.2
  905.4 98.3 %reshape.127 = bf16[8,4,128,8192,1]{3,2,1,0,4:T(8,128)(2,1)} reshape(bf16[32,128,16,512]{3,2,1,0:T(8,128)(2,1)} %get-tuple-element.9) | data formatting | bytes 134217728 | tf_op jit(solution)/shard_map/reshape | solution.py:79
  1003.7 33.2 %fusion = f32[2,8,8192]{2,0,1:T(2,128)S(1)} fusion(f32[8,128,8192]{2,1,0:T(8,128)} %convert_element_type.32, bf16[8,4,128,8192,1]{3,2,1,0,4:T(8,128)(2,1)} %reshape.127, bf16[2,8,128,4,128]{4,2,3,0,1:T(8,128)(2,1)S(1)} %copy.18), kind=kOutput, calls=%fused_computation.3 | convolution fusion | flops 17213292544 | bytes 103284736 | tf_op jit(solution)/shard_map/vabmn,abnp->vamp/dot_general | solution.py:83
  1044.6 120.7 %all-reduce.4.cloned.1.call-done = f32[2,32,512]{2,0,1:T(2,128)} async-done(((f32[2,32,512]{2,0,1:T(2,128)}), f32[2,32,512]{2,0,1:T(2,128)}) %all-reduce.4.cloned.1.call-update) | async-done | bytes 131088
  (152 shorter events, 181.1 us)
Async XLA Ops:
  7.2 5.1 copy-start.1
  7.2 41.1 %all-gather.9.cloned.1.call-start = ((), (), s32[]{:S(2)}) async-start(), calls=%async_computation.1 | async-start | bytes 5242880 | tf_op jit(solution)/shard_map/all_gather | solution.py:49
  8.2 6.1 copy-start.2
  10.9 267.3 %all-gather.7.cloned.1.call-start = ((), (), s32[]{:S(2)}) async-start(), calls=%async_computation | async-start | bytes 18874368 | tf_op jit(solution)/shard_map/all_gather | solution.py:45
  13.8 389.6 %all-gather.13.cloned.1.call-start = ((), (), s32[]{:S(2)}) async-start(), calls=%async_computation.3 | async-start | bytes 9437184 | tf_op jit(solution)/shard_map/all_gather | solution.py:56
  15.4 446.5 %all-gather.11.cloned.1.call-start = ((), (), s32[]{:S(2)}) async-start(), calls=%async_computation.2 | async-start | bytes 10485760 | tf_op jit(solution)/shard_map/all_gather | solution.py:53
  292.8 372.1 %all-gather.15.cloned.1.call-start = ((), (), s32[]{:S(2)}) async-start(), calls=%async_computation.4 | async-start | bytes 41943040 | tf_op jit(solution)/shard_map/all_gather | solution.py:13
  300.0 0.7 copy-start.3
  300.0 865.2 %all-reduce.4.cloned.1.call-start = ((), (), s32[]{:S(2)}) async-start(), calls=%async_computation.5 | async-start | bytes 262144
  475.7 2.4 copy-start
Sparse Core Ops, SparseCore 0:
  11.0 37.2 all-gather.8
  50.9 227.2 all-gather.6
  280.3 123.1 all-gather.12
  405.4 56.4 all-gather.10
  463.3 201.4 all-gather.14
  1040.8 124.4 all-reduce.3
